TPU v7x, 512 devices: a whole 4x8x8 slice. The times are simulated.
512 devices in a mesh: prow: 32 (over y, x), pcol: 8 (over z), zgrid: 2 (over core).
Axes of the slice: x: 4, y: 8, z: 8, core: 2. Of those that a mesh axis runs over, the one named last changes fastest.
Arguments:
- blocks: bfloat16 [32, 8, 2, 3, 40, 128, 128], P('prow', 'pcol', 'zgrid'), may hold values from -0.078125 to 0.078125
- sources: int32 [32, 8, 2, 3, 40], P('prow', 'pcol', 'zgrid'), may hold values from 0 to 7, as said below
- targets: int32 [32, 8, 2, 3, 40], P('prow', 'pcol', 'zgrid'), may hold values from 0 to 95, as said below
- counts: int32 [32, 8, 2, 3], P('prow', 'pcol', 'zgrid'), may hold values from 1 to 40, as said below
- given_sub: bfloat16 [32, 8, 2, 2, 128, 128], P('prow', 'pcol', 'zgrid'), may hold values from -6 to 6
- given_top: bfloat16 [32, 8, 2, 128, 128], P('prow', 'pcol'), may hold values from -6 to 6
- inverse_sub: bfloat16 [32, 8, 2, 2, 128, 128], P('prow', 'pcol', 'zgrid'), as said below
- inverse_top: bfloat16 [32, 8, 2, 128, 128], P('prow', 'pcol'), as said below
Outputs:
- solved_sub: bfloat16 [32, 8, 2, 2, 128, 128], P('prow', 'pcol', 'zgrid')
- solved_top: bfloat16 [32, 8, 2, 128, 128], P('prow', 'pcol')
Inputs may be any that keep to these rules, and one draw needn't show every extreme that they name: `sources`: column of the source supernode of a slot. `targets`: a slot of source level l aims at a level t = value // 32 + 1 above l and the row value % 32. `counts`: on some device of each source level all 40 slots are live. `inverse_sub`: unit lower triangular. `inverse_top`: unit lower triangular.
All inputs are finite; a program needn't handle non-finite values.
Results may differ from a plain program's by a relative error of at most 0.023.
Values may be sent and summed in bfloat16 or wider, within the bound.
A program may use at most 64 MiB of HBM per device.

v0:
```python
import jax
import jax.numpy as jnp
from jax import lax
from jax.sharding import PartitionSpec as P

slot_group = 8


def solve_block(inverse, residual):
    return jnp.dot(inverse, residual, preferred_element_type=jnp.float32).astype(jnp.bfloat16)


def spread_updates(totals, solved, block_set, source_ids, target_ids, live_count):
    gathered = lax.all_gather(solved[None], "pcol", axis=0, tiled=True)
    group_count = (live_count + slot_group - 1) // slot_group

    def add_group(position, running):
        first_slot = position * slot_group
        block_piece = lax.dynamic_slice_in_dim(block_set, first_slot, slot_group, 0)
        source_part = lax.dynamic_slice_in_dim(source_ids, first_slot, slot_group, 0)
        target_part = lax.dynamic_slice_in_dim(target_ids, first_slot, slot_group, 0)
        chosen = jnp.take(gathered, source_part, axis=0)
        product = jnp.einsum(
            "swk,skr->swr", block_piece, chosen, preferred_element_type=jnp.float32
        )
        alive_mask = first_slot + jnp.arange(slot_group) < live_count
        product = product * alive_mask.astype(jnp.float32)[:, None, None]
        return running.at[target_part].add(product)

    return lax.fori_loop(0, group_count, add_group, totals)


def reduce_rows(totals, level_index, row_count):
    section = lax.slice_in_dim(
        totals, level_index * row_count, (level_index + 1) * row_count, axis=0
    )
    return lax.psum_scatter(
        section.astype(jnp.bfloat16), "prow", scatter_dimension=0, tiled=True
    ).astype(jnp.float32)[0]


def ancestor_solve(incoming, given, inverse):
    merged = lax.psum(incoming.astype(jnp.bfloat16), "zgrid").astype(jnp.float32)
    residual = (given.astype(jnp.float32) - merged).astype(jnp.bfloat16)
    return solve_block(inverse, residual)


def local(blocks, sources, targets, counts, given_sub, given_top, inverse_sub, inverse_top):
    block_set = blocks[0, 0, 0]
    source_ids = sources[0, 0, 0]
    target_ids = targets[0, 0, 0]
    live_counts = counts[0, 0, 0]
    right_sub = given_sub[0, 0, 0]
    right_top = given_top[0, 0]
    factor_sub = inverse_sub[0, 0, 0]
    factor_top = inverse_top[0, 0]
    row_count = lax.axis_size("prow")
    totals = jnp.zeros((3 * row_count,) + right_sub.shape[1:], jnp.float32)
    level_zero = solve_block(factor_sub[0], right_sub[0])
    totals = spread_updates(
        totals, level_zero, block_set[0], source_ids[0], target_ids[0], live_counts[0]
    )
    incoming = reduce_rows(totals, 0, row_count)
    level_one = solve_block(
        factor_sub[1], (right_sub[1].astype(jnp.float32) - incoming).astype(jnp.bfloat16)
    )
    totals = spread_updates(
        totals, level_one, block_set[1], source_ids[1], target_ids[1], live_counts[1]
    )
    level_two = ancestor_solve(reduce_rows(totals, 1, row_count), right_top[0], factor_top[0])
    totals = spread_updates(
        totals, level_two, block_set[2], source_ids[2], target_ids[2], live_counts[2]
    )
    level_three = ancestor_solve(reduce_rows(totals, 2, row_count), right_top[1], factor_top[1])
    solved_sub = jnp.stack([level_zero, level_one])[None, None, None]
    solved_top = jnp.stack([level_two, level_three])[None, None]
    return (solved_sub, solved_top)


def solution(mesh):
    in_specs = (
        P("prow", "pcol", "zgrid", None, None, None, None),
        P("prow", "pcol", "zgrid", None, None),
        P("prow", "pcol", "zgrid", None, None),
        P("prow", "pcol", "zgrid", None),
        P("prow", "pcol", "zgrid", None, None, None),
        P("prow", "pcol", None, None, None),
        P("prow", "pcol", "zgrid", None, None, None),
        P("prow", "pcol", None, None, None),
    )
    out_specs = (P("prow", "pcol", "zgrid", None, None, None), P("prow", "pcol", None, None, None))
    return jax.shard_map(local, mesh=mesh, in_specs=in_specs, out_specs=out_specs, check_vma=False)
```

profile of v0, /device:TPU:1, one launch (start us, length us, event | category | flops | bytes accessed | tf_op | source)
XLA Modules:
  0.0 845.1 jit_solution(6969455676036020639)
XLA Ops:
  7.2 0.0 reduce-scatter.4.cloned.1.call-start
  7.3 1.4 fusion.42
  9.2 4.2 slice_bitcast_fusion
  13.4 0.1 convolution_convert_fusion.3
  13.5 25.9 %all-gather = bf16[1024,128]{1,0:T(8,128)(2,1)S(1)} all-gather(bf16[128,128]{1,0:T(8,128)(2,1)S(1)} %convolution_convert_fusion.3), channel_id=2, replica_groups=mesh['prow'=32,'pcol'=8,'zgrid'=2] {'pcol'}, dimensions={0}, use_global_device_ids=true | all-gather | bytes 294912 | tf_op jit(solution)/shard_map/all_gather | solution.py:14
  39.5 3.4 broadcast_in_dim.33
  42.9 10.6 %while.30 = (s32[]{:T(128)}, f32[96,128,128]{2,1,0:T(8,128)}, s32[]{:T(128)}, s32[40]{0:T(128)S(1)}, bf16[40,128,128]{2,1,0:T(8,128)(2,1)}, /*index=5*/s32[40]{0...) while((s32[]{:T(128)}, f32[96,128,128]{2,1,0:T(8,128)}, ...), condition=%wide.region_2.4_spmd, body=%wide.region_0.3_spmd.sunk | while | flops 33948772 | bytes 3150311 | solution.py:30
  42.9 0.6 compare_and_fusion.6
  43.6 0.6 gather_fusion
  44.2 1.3 convolution_multiply_fusion.6
  45.5 0.1 compare_select_fusion.12
  45.5 2.7 scatter_fusion
  48.2 0.6 compare_and_fusion.6
  48.9 0.6 gather_fusion
  49.5 1.3 convolution_multiply_fusion.6
  50.8 0.1 compare_select_fusion.12
  50.8 2.7 scatter_fusion
  53.6 2.8 slice.170
  56.4 0.0 reduce-scatter.4.cloned.1.call-update
  56.4 0.0 reduce-scatter.6.cloned.1.call-start
  57.1 232.8 %reduce-scatter.4.cloned.1.call-done = bf16[1,128,128]{2,1,0:T(8,128)(2,1)} async-done(((bf16[32,128,128]{2,1,0:T(8,128)(2,1)}), bf16[1,128,128]{2,1,0:T(8,128)(2,1)}) %reduce-scatter.4.cloned.1.call-update) | async-done | bytes 32784 | tf_op jit(solution)/shard_map/reduce_scatter | solution.py:37
  289.8 0.9 convolution_convert_fusion
  290.7 20.6 %all-gather.1 = bf16[1024,128]{1,0:T(8,128)(2,1)S(1)} all-gather(bf16[128,128]{1,0:T(8,128)(2,1)S(1)} %bitcast.81), channel_id=3, replica_groups=mesh['prow'=32,'pcol'=8,'zgrid'=2] {'pcol'}, dimensions={0}, use_global_device_ids=true | all-gather | bytes 294912 | tf_op jit(solution)/shard_map/all_gather | solution.py:14
  311.3 5.5 while.31
  311.3 0.7 compare_and_fusion.7
  312.1 0.6 gather_fusion.1
  312.7 1.3 convolution_multiply_fusion.7
  313.9 0.1 compare_select_fusion.13
  314.0 2.8 scatter_fusion.1
  316.8 2.8 slice.169
  319.6 0.0 reduce-scatter.8.cloned.1.call-start
  320.3 240.9 %reduce-scatter.6.cloned.1.call-done = bf16[1,128,128]{2,1,0:T(8,128)(2,1)} async-done(((bf16[32,128,128]{2,1,0:T(8,128)(2,1)}), bf16[1,128,128]{2,1,0:T(8,128)(2,1)}) %reduce-scatter.6.cloned.1.call-update) | async-done | bytes 32784 | tf_op jit(solution)/shard_map/reduce_scatter | solution.py:37
  561.2 9.5 %psum.14 = bf16[128,128]{1,0:T(8,128)(2,1)S(1)} all-reduce(bf16[128,128]{1,0:T(8,128)(2,1)} %bitcast.85), channel_id=1, replica_groups=mesh['prow'=32,'pcol'=8,'zgrid'=2] {'zgrid'}, use_global_device_ids=true, to_apply=%region_8.10 | all-reduce | flops 16384 | bytes 65536 | tf_op jit(solution)/shard_map/psum | solution.py:43
  570.7 0.2 convolution_convert_fusion.2
  570.9 20.1 %all-gather.2 = bf16[1024,128]{0,1:T(8,128)(2,1)S(1)} all-gather(bf16[128,128]{0,1:T(8,128)(2,1)S(1)} %bitcast.83), channel_id=4, replica_groups=mesh['prow'=32,'pcol'=8,'zgrid'=2] {'pcol'}, dimensions={0}, use_global_device_ids=true | all-gather | bytes 294912 | tf_op jit(solution)/shard_map/all_gather | solution.py:14
  591.1 0.2 copy.14
  591.2 4.5 while.32
  591.3 0.7 compare_and_fusion.8
  592.0 0.6 gather_fusion.2
  592.6 0.3 convolution_multiply_fusion.8
  592.9 0.1 compare_select_fusion.14
  593.0 2.7 scatter_fusion.2
  595.7 2.8 slice.168
  598.5 0.6 maximum_bitcast_fusion
  599.1 228.8 %reduce-scatter.8.cloned.1.call-done = bf16[1,128,128]{2,1,0:T(8,128)(2,1)} async-done(((bf16[32,128,128]{2,1,0:T(8,128)(2,1)}), bf16[1,128,128]{2,1,0:T(8,128)(2,1)}) %reduce-scatter.8.cloned.1.call-update) | async-done | bytes 32784 | tf_op jit(solution)/shard_map/reduce_scatter | solution.py:37
  827.9 9.7 %psum.15 = bf16[128,128]{1,0:T(8,128)(2,1)S(1)} all-reduce(bf16[128,128]{1,0:T(8,128)(2,1)} %bitcast.86), channel_id=1, replica_groups=mesh['prow'=32,'pcol'=8,'zgrid'=2] {'zgrid'}, use_global_device_ids=true, to_apply=%region_13.15 | all-reduce | flops 16384 | bytes 65536 | tf_op jit(solution)/shard_map/psum | solution.py:43
  837.6 0.2 fusion.18
  837.8 0.7 copy.12
  (20 shorter events, 0.1 us)
Async XLA Ops:
  7.2 6.2 copy-start
  7.2 6.2 copy-start.1
  7.2 32.3 %copy-start.4 = (s32[1,1,1,3,40]{4,2,3,1,0:T(1,128)S(1)}, s32[1,1,1,3,40]{4,2,3,1,0:T(1,128)}, u32[]{:S(2)}) copy-start(s32[1,1,1,3,40]{4,2,3,1,0:T(1,128)} %param.17) | copy-start | bytes 1444
  7.2 32.3 %copy-start.5 = (s32[1,1,1,3,40]{4,2,3,1,0:T(1,128)S(1)}, s32[1,1,1,3,40]{4,2,3,1,0:T(1,128)}, u32[]{:S(2)}) copy-start(s32[1,1,1,3,40]{4,2,3,1,0:T(1,128)} %param.18) | copy-start | bytes 1444
  7.2 282.6 %reduce-scatter.4.cloned.1.call-start = ((), (), s32[]{:S(2)}) async-start(), calls=%async_computation.3 | async-start | bytes 1081344 | tf_op jit(solution)/shard_map/reduce_scatter | solution.py:37
  56.4 504.8 %reduce-scatter.6.cloned.1.call-start = ((), (), s32[]{:S(2)}) async-start(), calls=%async_computation.4 | async-start | bytes 1081344 | tf_op jit(solution)/shard_map/reduce_scatter | solution.py:37
  311.3 259.4 %copy-start.2 = (bf16[1,1,2,128,128]{4,3,2,1,0:T(8,128)(2,1)S(1)}, bf16[1,1,2,128,128]{4,3,2,1,0:T(8,128)(2,1)}, u32[]{:S(2)}) copy-start(bf16[1,1,2,128,128]{4,3,2,1,0:T(8,128)(2,1)} %param.23) | copy-start | bytes 196612
  311.3 259.4 %copy-start.3 = (bf16[1,1,2,128,128]{4,3,2,1,0:T(8,128)(2,1)S(1)}, bf16[1,1,2,128,128]{4,3,2,1,0:T(8,128)(2,1)}, u32[]{:S(2)}) copy-start(bf16[1,1,2,128,128]{4,3,2,1,0:T(8,128)(2,1)} %param.21) | copy-start | bytes 196612
  319.6 508.4 %reduce-scatter.8.cloned.1.call-start = ((), (), s32[]{:S(2)}) async-start(), calls=%async_computation.5 | async-start | bytes 1081344 | tf_op jit(solution)/shard_map/reduce_scatter | solution.py:37
Sparse Core Ops, SparseCore 0:
  56.5 233.2 reduce-scatter.3
  319.7 241.4 reduce-scatter.5
  598.6 229.3 reduce-scatter.7
where the time goes:
time: 847 us; the launch traced here: 845 us
  waiting for transfers between devices  703 us (83%)
  blocking collectives  85.9 us (10%)
  local copies, waits for them, and re-layouts  20.6 us (2%)
  between operations  15.8 us (2%)
  other arithmetic  14.6 us (2%)
    reduce_scatter x3, waiting for transfers between devices, reduce_rows(): lax.psum_scatter(section.astype(jnp.bfloat16), 'prow', scatter_dimension=...  702 us
    all_gather x3, blocking collectives, spread_updates(): gathered = lax.all_gather(solved[None], 'pcol', axis=0, tiled=True)  66.7 us
    psum x2, blocking collectives, ancestor_solve(): lax.psum(incoming.astype(jnp.bfloat16), 'zgrid').astype(jnp.float32)  19.2 us
  transfers between devices with their start and end apart: 3, of which 3 were waited for; matrix products, arithmetic and copies ran while one was open for 0% of the time, Pallas kernels for 0%

commit v1 on v0

v1 whole, which is shorter than its diff:
```python
import functools

import jax
import jax.numpy as jnp
from jax import lax
from jax.experimental import pallas as pl
from jax.experimental.pallas import tpu as pltpu
from jax.sharding import PartitionSpec as P

MESH = pl.DeviceIdType.MESH
X_CHIPS = 4


def index_table(sources, targets, counts, rows):
    levels, cap = targets.shape
    slots = levels * cap
    order = jnp.arange(slots, dtype=jnp.int32)
    live = (order % cap) < jnp.repeat(counts, cap)
    key = jnp.where(live, targets.reshape(-1), -1)
    wanted = jnp.concatenate(
        [jnp.where(live, key, -2), jnp.arange(levels * rows, dtype=jnp.int32)]
    )
    limit = jnp.concatenate(
        [order, jnp.repeat((jnp.arange(levels, dtype=jnp.int32) + 1) * cap, rows)]
    )
    hit = (wanted[:, None] == key[None, :]) & (order[None, :] < limit[:, None])
    found = jnp.max(jnp.where(hit, order[None, :], -1), axis=1)
    found = jnp.where(found < 0, slots, found)
    return jnp.concatenate([sources.reshape(-1), found])


def drain(ref, sem):
    pltpu.make_async_copy(ref, ref, sem).wait()


def kernel(
    sizes, table, blocks, given_sub, given_top, inverse_sub, inverse_top,
    out_sub, out_top,
    block_v, given_v, inverse_v, run, gathered_0, gathered_1, gathered_2,
    sums_1, xa_1, ya_in_1, ya_1, yb_1, xb_in_1, xb_1,
    give_t, take_t, sums_t, xa_t, ya_in_t, ya_t, yb_t, xb_in_t, xb_t, half_t, other_t,
    load_sem, small_sem, send_sem, recv_sem,
):
    nx, ny, nc, cap, width, sides, cut_1, cut_t = sizes
    rows = nx * ny
    half = width // 2
    slots = 3 * cap
    gathered = (gathered_0, gathered_1, gathered_2)
    p = lax.axis_index("prow")
    c = lax.axis_index("pcol")
    k = lax.axis_index("zgrid")
    x = lax.rem(p, nx)
    y = lax.div(p, nx)

    def x_peer(d):
        return {"prow": y * nx + lax.rem(x + d, nx)}

    def y_peer(d):
        return {"prow": lax.rem(y + d, ny) * nx + x}

    def z_peer(d):
        return {"pcol": lax.rem(c + d, nc)}

    core = {"zgrid": 1 - k}
    x_order = [d for d in (2, 1, nx - 1) if 0 < d < nx][: nx - 1]
    x_order = list(dict.fromkeys(x_order))
    y_order = sorted(range(1, ny), key=lambda d: -min(d, ny - d))
    z_order = sorted(range(1, nc), key=lambda d: -min(d, nc - d))

    def send(src, dst, slot, device):
        pltpu.make_async_remote_copy(
            src_ref=src, dst_ref=dst, send_sem=send_sem.at[slot], recv_sem=recv_sem.at[slot],
            device_id=device, device_id_type=MESH,
        ).start()

    loads = [pltpu.make_async_copy(blocks.at[l], block_v.at[l], load_sem.at[l]) for l in range(3)]
    smalls = []
    for j in range(4):
        g = given_sub.at[j] if j < 2 else given_top.at[j - 2]
        i = inverse_sub.at[j] if j < 2 else inverse_top.at[j - 2]
        smalls.append(pltpu.make_async_copy(g, given_v.at[j], small_sem.at[2 * j]))
        smalls.append(pltpu.make_async_copy(i, inverse_v.at[j], small_sem.at[2 * j + 1]))
    for s in smalls[:2]:
        s.start()
    loads[0].start()
    for s in smalls[2:]:
        s.start()
    loads[1].start()
    loads[2].start()

    barrier = pltpu.get_barrier_semaphore()
    partners = (
        [x_peer(d) for d in x_order] + [y_peer(d) for d in y_order]
        + [z_peer(d) for d in z_order] + [core]
    )
    for device in partners:
        pl.semaphore_signal(barrier, inc=1, device_id=device, device_id_type=MESH)

    run[slots] = jnp.zeros((width, sides), jnp.float32)
    for s in smalls:
        s.wait()

    def solve(l, residual):
        return jnp.dot(
            inverse_v[l], residual, preferred_element_type=jnp.float32
        ).astype(jnp.bfloat16)

    def share(l, solved):
        held = gathered[l]
        held[c] = solved
        for d in z_order:
            send(held.at[c], held.at[c], l, z_peer(d))

    def products(l):
        held = gathered[l]
        drain(held.at[pl.ds(0, nc - 1)], recv_sem.at[l])
        loads[l].wait()
        group = 4

        def step(i, carry):
            base = i * group
            values = [
                jnp.dot(
                    block_v[l, base + u], held[table[l * cap + base + u]],
                    preferred_element_type=jnp.float32,
                )
                for u in range(group)
            ]
            for u in range(group):
                s = l * cap + base + u
                run[s] = values[u] + run[table[slots + s]]
            return carry

        lax.fori_loop(0, cap // group, step, 0)

    def total(l, row):
        return run[table[2 * slots + l * rows + row]]

    def reduce_rows(sums, height, cut, xa, ya_in, ya, yb, xb_in, xb, base):
        low = pl.ds(0, cut)
        high = pl.ds(cut, height - cut)
        for d in x_order:
            to = lax.rem(x + d, nx)
            send(sums.at[to, :, low], xa.at[d - 1], base, x_peer(d))
        for d in y_order:
            to = lax.rem(y + d, ny)
            send(sums.at[:, to, high], yb.at[d - 1], base + 1, y_peer(d))
        drain(xa, recv_sem.at[base])

        def add_x(j, carry):
            value = sums[x, j, low].astype(jnp.float32)
            for d in range(nx - 1):
                value = value + xa[d, j].astype(jnp.float32)
            ya_in[j] = value.astype(jnp.bfloat16)
            return carry

        lax.fori_loop(0, ny, add_x, 0)
        for d in y_order:
            send(ya_in.at[lax.rem(y + d, ny)], ya.at[d - 1], base + 2, y_peer(d))
        drain(yb, recv_sem.at[base + 1])

        def add_y(j, carry):
            value = sums[j, y, high].astype(jnp.float32)
            for d in range(ny - 1):
                value = value + yb[d, j].astype(jnp.float32)
            xb_in[j] = value.astype(jnp.bfloat16)
            return carry

        lax.fori_loop(0, nx, add_y, 0)
        for d in x_order:
            send(xb_in.at[lax.rem(x + d, nx)], xb.at[d - 1], base + 3, x_peer(d))
        drain(xb, recv_sem.at[base + 3])
        upper = xb_in[x].astype(jnp.float32)
        for d in range(nx - 1):
            upper = upper + xb[d].astype(jnp.float32)
        drain(ya, recv_sem.at[base + 2])
        lower = ya_in[y].astype(jnp.float32)
        for d in range(ny - 1):
            lower = lower + ya[d].astype(jnp.float32)
        return lower, upper

    pl.semaphore_wait(barrier, len(partners))

    level_zero = solve(0, given_v[0])
    share(0, level_zero)
    out_sub[0] = level_zero
    products(0)

    def place_1(j, carry):
        sums_1[lax.rem(j, nx), lax.div(j, nx)] = total(0, j).astype(jnp.bfloat16)
        return carry

    lax.fori_loop(0, rows, place_1, 0)
    lower, upper = reduce_rows(sums_1, width, cut_1, xa_1, ya_in_1, ya_1, yb_1, xb_in_1, xb_1, 3)
    incoming = jnp.concatenate([lower, upper], axis=0)
    level_one = solve(1, (given_v[1].astype(jnp.float32) - incoming).astype(jnp.bfloat16))
    share(1, level_one)
    out_sub[1] = level_one
    products(1)

    mine = pl.ds(pl.multiple_of(k * half, half), half)
    theirs = pl.ds(pl.multiple_of((1 - k) * half, half), half)

    def ancestor(l):
        t = l - 1
        base = 7 + 6 * t

        def place(j, carry):
            give_t[t, lax.rem(j, nx), lax.div(j, nx)] = run[
                table[2 * slots + l * rows + j], theirs
            ].astype(jnp.bfloat16)
            return carry

        lax.fori_loop(0, rows, place, 0)
        send(give_t.at[t], take_t.at[t], base, core)
        drain(take_t.at[t], recv_sem.at[base])

        def merge(j, carry):
            i, m = lax.rem(j, nx), lax.div(j, nx)
            value = run[table[2 * slots + l * rows + j], mine]
            sums_t[t, i, m] = (value + take_t[t, i, m].astype(jnp.float32)).astype(jnp.bfloat16)
            return carry

        lax.fori_loop(0, rows, merge, 0)
        lower, upper = reduce_rows(
            sums_t.at[t], half, cut_t, xa_t.at[t], ya_in_t.at[t], ya_t.at[t],
            yb_t.at[t], xb_in_t.at[t], xb_t.at[t], base + 1,
        )
        incoming = jnp.concatenate([lower, upper], axis=0)
        residual = given_v[l + 1, mine].astype(jnp.float32) - incoming
        half_t[t, mine] = residual.astype(jnp.bfloat16)
        send(half_t.at[t, mine], other_t.at[t], base + 5, core)
        drain(other_t.at[t], recv_sem.at[base + 5])
        half_t[t, theirs] = other_t[t]
        return solve(l + 1, half_t[t])

    level_two = ancestor(1)
    share(2, level_two)
    out_top[0] = level_two
    products(2)
    level_three = ancestor(2)
    out_top[1] = level_three

    for l in range(3):
        drain(gathered[l].at[pl.ds(0, nc - 1)], send_sem.at[l])
    for refs, base in (
        ((xa_1, yb_1, ya_1, xb_1), 3),
        ((take_t.at[0], xa_t.at[0], yb_t.at[0], ya_t.at[0], xb_t.at[0], other_t.at[0]), 7),
        ((take_t.at[1], xa_t.at[1], yb_t.at[1], ya_t.at[1], xb_t.at[1], other_t.at[1]), 13),
    ):
        for j, ref in enumerate(refs):
            drain(ref, send_sem.at[base + j])


def local(nx, axis_sizes, blocks, sources, targets, counts, given_sub, given_top, inverse_sub, inverse_top):
    rows, nc = axis_sizes
    ny = rows // nx
    levels, cap, width = blocks.shape[3:6]
    sides = given_sub.shape[-1]
    half = width // 2
    cut_1 = width * 3 // 4
    cut_t = half * 3 // 4
    table = index_table(sources[0, 0, 0], targets[0, 0, 0], counts[0, 0, 0], rows)
    sizes = (nx, ny, nc, cap, width, sides, cut_1, cut_t)
    bf16 = jnp.bfloat16

    def exchange(lead, height, cut):
        rest = height - cut
        return [
            pltpu.VMEM(lead + (nx - 1, ny, cut, sides), bf16),
            pltpu.VMEM(lead + (ny, cut, sides), bf16),
            pltpu.VMEM(lead + (ny - 1, cut, sides), bf16),
            pltpu.VMEM(lead + (ny - 1, nx, rest, sides), bf16),
            pltpu.VMEM(lead + (nx, rest, sides), bf16),
            pltpu.VMEM(lead + (nx - 1, rest, sides), bf16),
        ]

    anywhere = pl.BlockSpec(memory_space=pltpu.HBM)
    vmem = pl.BlockSpec(memory_space=pltpu.VMEM)
    solved_sub, solved_top = pl.pallas_call(
        functools.partial(kernel, sizes),
        out_shape=(
            jax.ShapeDtypeStruct((2, width, sides), bf16),
            jax.ShapeDtypeStruct((2, width, sides), bf16),
        ),
        in_specs=[pl.BlockSpec(memory_space=pltpu.SMEM)] + [anywhere] * 5,
        out_specs=(vmem, vmem),
        scratch_shapes=[
            pltpu.VMEM((levels, cap, width, width), bf16),
            pltpu.VMEM((4, width, sides), bf16),
            pltpu.VMEM((4, width, width), bf16),
            pltpu.VMEM((levels * cap + 1, width, sides), jnp.float32),
            pltpu.VMEM((nc, width, sides), bf16),
            pltpu.VMEM((nc, width, sides), bf16),
            pltpu.VMEM((nc, width, sides), bf16),
            pltpu.VMEM((nx, ny, width, sides), bf16),
            *exchange((), width, cut_1),
            pltpu.VMEM((2, nx, ny, half, sides), bf16),
            pltpu.VMEM((2, nx, ny, half, sides), bf16),
            pltpu.VMEM((2, nx, ny, half, sides), bf16),
            *exchange((2,), half, cut_t),
            pltpu.VMEM((2, width, sides), bf16),
            pltpu.VMEM((2, half, sides), bf16),
            pltpu.SemaphoreType.DMA((3,)),
            pltpu.SemaphoreType.DMA((8,)),
            pltpu.SemaphoreType.DMA((19,)),
            pltpu.SemaphoreType.DMA((19,)),
        ],
        compiler_params=pltpu.CompilerParams(
            collective_id=0, has_side_effects=True, vmem_limit_bytes=60 * 1024 * 1024
        ),
        name="substitution",
    )(
        table, blocks[0, 0, 0], given_sub[0, 0, 0], given_top[0, 0],
        inverse_sub[0, 0, 0], inverse_top[0, 0],
    )
    return solved_sub[None, None, None], solved_top[None, None]


def solution(mesh):
    nx = X_CHIPS
    in_specs = (
        P("prow", "pcol", "zgrid", None, None, None, None),
        P("prow", "pcol", "zgrid", None, None),
        P("prow", "pcol", "zgrid", None, None),
        P("prow", "pcol", "zgrid", None),
        P("prow", "pcol", "zgrid", None, None, None),
        P("prow", "pcol", None, None, None),
        P("prow", "pcol", "zgrid", None, None, None),
        P("prow", "pcol", None, None, None),
    )
    out_specs = (P("prow", "pcol", "zgrid", None, None, None), P("prow", "pcol", None, None, None))
    body = functools.partial(local, nx, (mesh.shape["prow"], mesh.shape["pcol"]))
    return jax.shard_map(body, mesh=mesh, in_specs=in_specs, out_specs=out_specs, check_vma=False)
```

time: 847 us -> 100 us (0.12)
  waiting for transfers between devices: 703 us -> 0 us
  Pallas kernels: 0 us -> 92.8 us
  blocking collectives: 85.9 us -> 0 us
  local copies, waits for them, and re-layouts: 20.6 us -> 4.09 us
  between operations: 15.8 us -> 0.68 us
  other arithmetic: 14.6 us -> 2.36 us
    reduce_scatter x3 -> x0, waiting for transfers between devices: 702 us -> none  [reduce_rows(): lax.psum_scatter(section.astype(jnp.bfloat16), 'prow', scatter_dimension=...]
    pallas_call x0 -> x1, Pallas kernels: none -> 92.8 us  [local(): pl.pallas_call(functools.partial(kernel, sizes), out_shape=(jax.ShapeDtyp...]
    all_gather x3 -> x0, blocking collectives: 66.7 us -> none  [spread_updates(): gathered = lax.all_gather(solved[None], 'pcol', axis=0, tiled=True)]
    psum x2 -> x0, blocking collectives: 19.2 us -> none  [ancestor_solve(): lax.psum(incoming.astype(jnp.bfloat16), 'zgrid').astype(jnp.float32)]
    scatter-add x4 -> x0, other arithmetic: 10.9 us -> none  [add_group(): return running.at[target_part].add(product)]
    slice x4 -> x0, local copies, waits for them, and re-layouts: 9.71 us -> none  [the longest x3 8.3 us: reduce_rows(): lax.slice_in_dim(totals, level_index * row_count, (level_index + 1) * row...]
  transfers between devices with their start and end apart: 3 -> 0, of which waited for: 3 -> 0; matrix products, arithmetic and copies ran while one was open for 0% -> 0% of each run, Pallas kernels for 0% -> 0%
where the time goes in v1:
time: 100 us; the launch traced here: 99.9 us
  Pallas kernels  92.8 us (93%)
  local copies, waits for them, and re-layouts  4.09 us (4%)
  other arithmetic  2.36 us (2%)
    pallas_call x1, Pallas kernels, local(): pl.pallas_call(functools.partial(kernel, sizes), out_shape=(jax.ShapeDtyp...  92.8 us
    unnamed x2, local copies, waits for them, and re-layouts  2.95 us

profile of v1, /device:TPU:1, one launch (start us, length us, event | category | flops | bytes accessed | tf_op | source)
XLA Modules:
  0.0 99.9 jit_solution(9313581377166861335)
XLA Ops:
  0.7 0.1 broadcast_in_dim.41
  0.7 0.1 reshape.32
  0.8 0.7 reduce
  1.5 0.1 reshape_squeeze.6
  1.6 0.7 reduce.1
  2.3 0.1 reshape_squeeze.7
  2.4 0.7 broadcast_in_dim.38
  3.1 0.1 reshape.31
  3.2 0.1 pad_add_fusion.1
  3.3 0.2 select_reduce_fusion
  3.5 0.7 pad_add_fusion.table
  4.2 92.8 %substitution.1 = (bf16[2,128,128]{2,1,0:T(8,128)(2,1)}, bf16[2,128,128]{2,1,0:T(8,128)(2,1)}) custom-call(s32[336]{0:T(512)} %pad_add_fusion.table, bf16[3,40,128,128]{3,2,1,0:T(8,128)(2,1)} %bitcast.8, bf16[2,128,128]{2,1,0:T(8,128)(2,1)} %bitcast.11, bf16[2,128,128]{2,1,0:T(8,128)(2,1)} %bitcast.12, bf16[2,128,128]{2,1,0:T(8,128)(2,1)} %bitcast.13, ...), custom_call_target="tpu_custom_call" | custom-call | tf_op jit(solution)/shard_map/substitution/pallas_call | solution.py:280
  97.0 1.5 %copy.12 = bf16[1,1,1,2,128,128]{5,4,3,2,1,0:T(8,128)(2,1)} copy(bf16[1,1,1,2,128,128]{5,4,3,2,1,0:T(8,128)(2,1)} %bitcast.10) | data formatting | bytes 131072
  98.5 1.5 %copy.13 = bf16[1,1,2,128,128]{4,3,2,1,0:T(8,128)(2,1)} copy(bf16[1,1,2,128,128]{4,3,2,1,0:T(8,128)(2,1)} %bitcast.9) | data formatting | bytes 131072
  (5 shorter events, 0.0 us)

commit v2 on v0

v2 whole, which is shorter than its diff:
```python
import functools

import jax
import jax.numpy as jnp
from jax import lax
from jax.experimental import pallas as pl
from jax.experimental.pallas import tpu as pltpu
from jax.sharding import PartitionSpec as P

MESH = pl.DeviceIdType.MESH
X_CHIPS = 4
PARTS = 2
LANES = 128
STEPS = ("g0", "x1", "y1", "g1", "c2", "x2", "y2", "g2", "f2", "c3", "x3", "y3", "f3")


def drain(ref, sem):
    pltpu.make_async_copy(ref, ref, sem).wait()


def times_transposed(left, right):
    return lax.dot_general(
        left, right, (((1,), (1,)), ((), ())), preferred_element_type=jnp.float32
    )


def kernel(
    sizes, sources, counts, targets, blocks, given_sub, given_top, inverse_sub, inverse_top,
    out_sub, out_top, key_v, table_v, table, block_v, given_v, given_t, inverse_v, run, top, *rest
):
    nx, ny, nc, cap, width, sides = sizes
    rows = nx * ny
    slots = 3 * cap
    part = sides // PARTS
    fine = part // 2
    gathered = [rest[PARTS * l : PARTS * (l + 1)] for l in range(3)]
    rest = rest[3 * PARTS :]
    sums, xa, y_in, ya = [[rest[4 * j + i] for j in range(3)] for i in range(4)]
    give, take, table_sem, load_sem, small_sem, send_sem, recv_sem = rest[12:]
    p = lax.axis_index("prow")
    c = lax.axis_index("pcol")
    k = lax.axis_index("zgrid")
    x = lax.rem(p, nx)
    y = lax.div(p, nx)

    def x_peer(d):
        return {"prow": y * nx + lax.rem(x + d, nx)}

    def y_peer(d):
        return {"prow": lax.rem(y + d, ny) * nx + x}

    def z_peer(d):
        return {"pcol": lax.rem(c + d, nc)}

    core = {"zgrid": 1 - k}
    x_order = sorted(range(1, nx), key=lambda d: -min(d, nx - d))
    y_order = sorted(range(1, ny), key=lambda d: -min(d, ny - d))
    z_order = sorted(range(1, nc), key=lambda d: -min(d, nc - d))
    pending = {}

    def sem_of(step, j):
        return STEPS.index(step) * PARTS + j

    def send(src, dst, step, j, device, everything):
        slot = sem_of(step, j)
        pending[slot] = everything
        pltpu.make_async_remote_copy(
            src_ref=src, dst_ref=dst, send_sem=send_sem.at[slot], recv_sem=recv_sem.at[slot],
            device_id=device, device_id_type=MESH,
        ).start()

    def arrive(step, j):
        slot = sem_of(step, j)
        drain(pending[slot], recv_sem.at[slot])

    def finish():
        for slot, everything in pending.items():
            drain(everything, send_sem.at[slot])

    loads = [pltpu.make_async_copy(blocks.at[l], block_v.at[l], load_sem.at[l]) for l in range(3)]
    smalls = []
    for n in range(4):
        g = given_sub.at[n] if n < 2 else given_top.at[n - 2]
        i = inverse_sub.at[n] if n < 2 else inverse_top.at[n - 2]
        smalls.append(pltpu.make_async_copy(g, given_v.at[n], small_sem.at[2 * n]))
        smalls.append(pltpu.make_async_copy(i, inverse_v.at[n], small_sem.at[2 * n + 1]))
    for s in smalls:
        s.start()
    for s in loads:
        s.start()

    barrier = pltpu.get_barrier_semaphore()
    partners = (
        [x_peer(d) for d in x_order] + [y_peer(d) for d in y_order]
        + [z_peer(d) for d in z_order] + [core]
    )
    for device in partners:
        pl.semaphore_signal(barrier, inc=1, device_id=device, device_id_type=MESH)

    lanes = lax.broadcasted_iota(jnp.int32, (1, LANES), 1)
    key_v[...] = jnp.full(key_v.shape, -1, jnp.int32)
    for l in range(3):
        live = lanes[:, :cap] < counts[0, l]
        key_v[l : l + 1, :cap] = jnp.where(live, targets[l], -1)
    key_rows = key_v[...]
    key_columns = key_rows.T
    line = lax.broadcasted_iota(jnp.int32, (LANES, LANES), 0)
    lane = lax.broadcasted_iota(jnp.int32, (LANES, LANES), 1)

    def latest(wanted, l, strict):
        best = jnp.full((1, LANES), -1, jnp.int32)
        for m in range(l + 1):
            hit = (key_columns[:, m : m + 1] == wanted) & (wanted >= 0)
            if m == l and strict:
                hit = hit & (line < lane)
            best = jnp.maximum(best, jnp.max(jnp.where(hit, line + m * cap, -1), axis=0, keepdims=True))
        return jnp.where(best < 0, slots, best)

    for l in range(3):
        table_v[l : l + 1] = latest(key_rows[l : l + 1], l, True)
        table_v[3 + l : 4 + l] = latest(lanes + l * rows, l, False)
    to_scalars = pltpu.make_async_copy(table_v, table, table_sem)
    to_scalars.start()
    run[slots] = jnp.zeros((sides, width), jnp.float32)
    for s in smalls:
        s.wait()
    for n in range(4):
        given_t[n] = given_v[n].astype(jnp.float32).T

    def natural(j, h):
        return pl.ds(h * part + j * fine, fine)

    def of_part(l, j):
        return jnp.concatenate([given_t[l, natural(j, h)] for h in range(2)], axis=0)

    def solve(l, residual):
        solved = times_transposed(residual.astype(jnp.bfloat16), inverse_v[l])
        return solved.astype(jnp.bfloat16)

    def share(l, j, solved):
        held = gathered[l][j]
        held[c] = solved
        for d in z_order:
            send(held.at[c], held.at[c], f"g{l}", j, z_peer(d), held.at[pl.ds(0, nc - 1)])

    def turn(l):
        loads[l].wait()

        def step(i, carry):
            for u in range(4):
                block_v[l, i * 4 + u] = block_v[l, i * 4 + u].T
            return carry

        lax.fori_loop(0, cap // 4, step, 0)

    def products(l, j):
        held = gathered[l][j]
        group = cap // 2 if cap % 2 == 0 else cap
        lines = pl.ds(j * part, part)

        def source(s):
            if l < 2:
                return held[s]
            return jnp.concatenate([held[0, s], held[1, s]], axis=0)

        def step(i, carry):
            base = i * group
            values = [
                jnp.dot(
                    source(sources[l, 0, base + u]), block_v[l, base + u],
                    preferred_element_type=jnp.float32,
                )
                for u in range(group)
            ]
            for u in range(group):
                s = l * cap + base + u
                run[s, lines] = values[u] + run[table[l, base + u], lines]
            return carry

        lax.fori_loop(0, cap // group, step, 0)

    def x_stage(l, j, value):
        kept = sums[l].at[j]
        for d in x_order:
            to = lax.rem(x + d, nx)

            def place(m, carry):
                kept[d - 1, m] = value(to, m).astype(jnp.bfloat16)
                return carry

            lax.fori_loop(0, ny, place, 0)
            send(kept.at[d - 1], xa[l].at[j, d - 1], f"x{l + 1}", j, x_peer(d), xa[l].at[j])

    def y_stage(l, j, value):
        arrive(f"x{l + 1}", j)

        def add(m, carry):
            total = value(x, m)
            for d in range(nx - 1):
                total = total + xa[l][j, d, m].astype(jnp.float32)
            y_in[l][j, m] = total.astype(jnp.bfloat16)
            return carry

        lax.fori_loop(0, ny, add, 0)
        for d in y_order:
            to = lax.rem(y + d, ny)
            send(y_in[l].at[j, to], ya[l].at[j, d - 1], f"y{l + 1}", j, y_peer(d), ya[l].at[j])

    def incoming(l, j):
        arrive(f"y{l + 1}", j)
        total = y_in[l][j, y].astype(jnp.float32)
        for d in range(ny - 1):
            total = total + ya[l][j, d].astype(jnp.float32)
        return total

    def own_value(l, lines):
        return lambda to, m: run[table[3 + l, m * nx + to], lines]

    def sub_lines(j):
        return pl.ds(j * part, part)

    def top_lines(j, h):
        return pl.ds(pl.multiple_of(j * part + h * fine, fine), fine)

    def merged(l, j):
        def value(to, m):
            own = run[table[3 + l, m * nx + to], top_lines(j, k)]
            return own + take[l - 1, j, m, to].astype(jnp.float32)

        return value

    def core_stage(l, j):
        kept = give.at[l - 1, j]

        def place(m, carry):
            for to in range(nx):
                kept[m, to] = run[table[3 + l, m * nx + to], top_lines(j, 1 - k)].astype(jnp.bfloat16)
            return carry

        lax.fori_loop(0, ny, place, 0)
        send(kept, take.at[l - 1, j], f"c{l + 1}", j, core, take.at[l - 1, j])

    def top_solve(l, j):
        lines = pl.ds(pl.multiple_of(k * part + j * fine, fine), fine)
        return solve(l + 1, given_t[l + 1, lines] - incoming(l, j))

    def emit(out, n, pieces):
        whole = jnp.concatenate(
            [pieces(j, h) for h in range(2) for j in range(PARTS)], axis=0
        )
        out[n] = whole.astype(jnp.float32).T.astype(jnp.bfloat16)

    to_scalars.wait()
    turn(0)
    pl.semaphore_wait(barrier, len(partners))

    parts = range(PARTS)
    for j in parts:
        share(0, j, solve(0, of_part(0, j)))
    for j in parts:
        arrive("g0", j)
        products(0, j)
        x_stage(0, j, own_value(0, sub_lines(j)))
    turn(1)
    for j in parts:
        y_stage(0, j, own_value(0, sub_lines(j)))
    for j in parts:
        share(1, j, solve(1, of_part(1, j) - incoming(0, j)))
    for j in parts:
        arrive("g1", j)
        products(1, j)
        core_stage(1, j)
    for j in parts:
        arrive("c2", j)
        x_stage(1, j, merged(1, j))
    turn(2)
    for j in parts:
        y_stage(1, j, merged(1, j))
    for j in parts:
        held = gathered[2][j]
        solved = top_solve(1, j)
        held[k, c] = solved
        for d in z_order:
            send(held.at[k, c], held.at[k, c], "g2", j, z_peer(d), held.at[0, pl.ds(0, nc - 1)])
    for j in parts:
        held = gathered[2][j]
        arrive("g2", j)
        send(held.at[k], held.at[k], "f2", j, core, held.at[0])
    for n in range(2):
        emit(out_sub, n, lambda j, h, n=n: gathered[n][j][c, pl.ds(h * fine, fine)])
    for j in parts:
        arrive("f2", j)
        products(2, j)
        core_stage(2, j)
    for j in parts:
        arrive("c3", j)
        x_stage(2, j, merged(2, j))
    for j in parts:
        y_stage(2, j, merged(2, j))
    emit(out_top, 0, lambda j, h: gathered[2][j][h, c])
    for j in parts:
        solved = top_solve(2, j)
        top[j, k] = solved
        send(top.at[j, k], top.at[j, k], "f3", j, core, top.at[j, 0])
    for j in parts:
        arrive("f3", j)
    emit(out_top, 1, lambda j, h: top[j, h])
    finish()


def local(nx, axis_sizes, blocks, sources, targets, counts, given_sub, given_top, inverse_sub, inverse_top):
    rows, nc = axis_sizes
    ny = rows // nx
    levels, cap, width = blocks.shape[3:6]
    sides = given_sub.shape[-1]
    part = sides // PARTS
    fine = part // 2
    sizes = (nx, ny, nc, cap, width, sides)
    bf16 = jnp.bfloat16

    def exchange(height):
        return [
            pltpu.VMEM((PARTS, nx - 1, ny, height, width), bf16),
            pltpu.VMEM((PARTS, nx - 1, ny, height, width), bf16),
            pltpu.VMEM((PARTS, ny, height, width), bf16),
            pltpu.VMEM((PARTS, ny - 1, height, width), bf16),
        ]

    smem = pl.BlockSpec(memory_space=pltpu.SMEM)
    anywhere = pl.BlockSpec(memory_space=pltpu.HBM)
    vmem = pl.BlockSpec(memory_space=pltpu.VMEM)
    semaphores = len(STEPS) * PARTS
    solved_sub, solved_top = pl.pallas_call(
        functools.partial(kernel, sizes),
        out_shape=(
            jax.ShapeDtypeStruct((2, width, sides), bf16),
            jax.ShapeDtypeStruct((2, width, sides), bf16),
        ),
        in_specs=[smem, smem, vmem] + [anywhere] * 5,
        out_specs=(vmem, vmem),
        scratch_shapes=[
            pltpu.VMEM((8, LANES), jnp.int32),
            pltpu.VMEM((8, LANES), jnp.int32),
            pltpu.SMEM((8, LANES), jnp.int32),
            pltpu.VMEM((levels, cap, width, width), bf16),
            pltpu.VMEM((4, width, sides), bf16),
            pltpu.VMEM((4, sides, width), jnp.float32),
            pltpu.VMEM((4, width, width), bf16),
            pltpu.VMEM((levels * cap + 1, sides, width), jnp.float32),
            pltpu.VMEM((PARTS, 2, fine, width), bf16),
            *[pltpu.VMEM((nc, part, width), bf16)] * (2 * PARTS),
            *[pltpu.VMEM((2, nc, fine, width), bf16)] * PARTS,
            *exchange(part),
            *exchange(fine),
            *exchange(fine),
            pltpu.VMEM((2, PARTS, ny, nx, fine, width), bf16),
            pltpu.VMEM((2, PARTS, ny, nx, fine, width), bf16),
            pltpu.SemaphoreType.DMA,
            pltpu.SemaphoreType.DMA((3,)),
            pltpu.SemaphoreType.DMA((8,)),
            pltpu.SemaphoreType.DMA((semaphores,)),
            pltpu.SemaphoreType.DMA((semaphores,)),
        ],
        compiler_params=pltpu.CompilerParams(
            collective_id=0, has_side_effects=True, vmem_limit_bytes=60 * 1024 * 1024
        ),
        name="substitution",
    )(
        sources.reshape(levels, 1, cap), counts.reshape(1, levels), targets.reshape(levels, 1, cap), blocks[0, 0, 0], given_sub[0, 0, 0], given_top[0, 0],
        inverse_sub[0, 0, 0], inverse_top[0, 0],
    )
    return solved_sub[None, None, None], solved_top[None, None]


def solution(mesh):
    nx = X_CHIPS
    in_specs = (
        P("prow", "pcol", "zgrid", None, None, None, None),
        P("prow", "pcol", "zgrid", None, None),
        P("prow", "pcol", "zgrid", None, None),
        P("prow", "pcol", "zgrid", None),
        P("prow", "pcol", "zgrid", None, None, None),
        P("prow", "pcol", None, None, None),
        P("prow", "pcol", "zgrid", None, None, None),
        P("prow", "pcol", None, None, None),
    )
    out_specs = (P("prow", "pcol", "zgrid", None, None, None), P("prow", "pcol", None, None, None))
    body = functools.partial(local, nx, (mesh.shape["prow"], mesh.shape["pcol"]))
    return jax.shard_map(body, mesh=mesh, in_specs=in_specs, out_specs=out_specs, check_vma=False)
```

time: 847 us -> 86 us (0.10)
  waiting for transfers between devices: 703 us -> 0 us
  blocking collectives: 85.9 us -> 0 us
  Pallas kernels: 0 us -> 82.2 us
  local copies, waits for them, and re-layouts: 20.6 us -> 2.95 us
  between operations: 15.8 us -> 0.64 us
  other arithmetic: 14.6 us -> 0 us
    reduce_scatter x3 -> x0, waiting for transfers between devices: 702 us -> none  [reduce_rows(): lax.psum_scatter(section.astype(jnp.bfloat16), 'prow', scatter_dimension=...]
    pallas_call x0 -> x1, Pallas kernels: none -> 82.2 us  [local(): pl.pallas_call(functools.partial(kernel, sizes), out_shape=(jax.ShapeDtyp...]
    all_gather x3 -> x0, blocking collectives: 66.7 us -> none  [spread_updates(): gathered = lax.all_gather(solved[None], 'pcol', axis=0, tiled=True)]
    psum x2 -> x0, blocking collectives: 19.2 us -> none  [ancestor_solve(): lax.psum(incoming.astype(jnp.bfloat16), 'zgrid').astype(jnp.float32)]
    scatter-add x4 -> x0, other arithmetic: 10.9 us -> none  [add_group(): return running.at[target_part].add(product)]
    slice x4 -> x0, local copies, waits for them, and re-layouts: 9.71 us -> none  [the longest x3 8.3 us: reduce_rows(): lax.slice_in_dim(totals, level_index * row_count, (level_index + 1) * row...]
  transfers between devices with their start and end apart: 3 -> 0, of which waited for: 3 -> 0; matrix products, arithmetic and copies ran while one was open for 0% -> 0% of each run, Pallas kernels for 0% -> 0%
where the time goes in v2:
time: 86 us; the launch traced here: 85.7 us
  Pallas kernels  82.2 us (96%)
  local copies, waits for them, and re-layouts  2.95 us (3%)
    pallas_call x1, Pallas kernels, local(): pl.pallas_call(functools.partial(kernel, sizes), out_shape=(jax.ShapeDtyp...  82.2 us
    unnamed x2, local copies, waits for them, and re-layouts  2.95 us

profile of v2, /device:TPU:1, one launch (start us, length us, event | category | flops | bytes accessed | tf_op | source)
XLA Modules:
  0.0 85.7 jit_solution(6519412746839884092)
XLA Ops:
  0.6 82.2 %substitution.1 = (bf16[2,128,128]{2,1,0:T(8,128)(2,1)}, bf16[2,128,128]{2,1,0:T(8,128)(2,1)}) custom-call(s32[3,1,40]{2,1,0:T(1,128)} %bitcast.17, s32[1,3]{1,0:T(1,128)} %bitcast.19, s32[3,1,40]{2,1,0:T(1,128)} %bitcast.18, bf16[3,40,128,128]{3,2,1,0:T(8,128)(2,1)} %bitcast.10, bf16[2,128,128]{2,1,0:T(8,128)(2,1)} %bitcast.11, ...), custom_call_target="tpu_custom_call" | custom-call | tf_op jit(solution)/shard_map/substitution/pallas_call | solution.py:333
  82.8 1.5 %copy.12 = bf16[1,1,1,2,128,128]{5,4,3,2,1,0:T(8,128)(2,1)} copy(bf16[1,1,1,2,128,128]{5,4,3,2,1,0:T(8,128)(2,1)} %bitcast.16) | data formatting | bytes 131072
  84.3 1.5 %copy.13 = bf16[1,1,2,128,128]{4,3,2,1,0:T(8,128)(2,1)} copy(bf16[1,1,2,128,128]{4,3,2,1,0:T(8,128)(2,1)} %bitcast.15) | data formatting | bytes 131072

commit v3 on v2

--- a/solution.py
+++ b/solution.py
@@ -11,7 +11,10 @@
 X_CHIPS = 4
 PARTS = 2
 LANES = 128
-STEPS = ("g0", "x1", "y1", "g1", "c2", "x2", "y2", "g2", "f2", "c3", "x3", "y3", "f3")
+STEPS = (
+    "g0", "x1", "v1", "y1", "w1", "g1", "c2", "x2", "v2", "y2", "w2", "g2", "f2",
+    "c3", "x3", "v3", "y3", "w3", "f3",
+)
 
 
 def drain(ref, sem):
@@ -25,8 +28,8 @@
 
 
 def kernel(
-    sizes, sources, counts, targets, blocks, given_sub, given_top, inverse_sub, inverse_top,
-    out_sub, out_top, key_v, table_v, table, block_v, given_v, given_t, inverse_v, run, top, *rest
+    sizes, sources_h, counts_h, targets_h, blocks, given_sub, given_top, inverse_sub, inverse_top,
+    out_sub, out_top, sources, counts, targets, index_sem, result, key_v, table_v, table, block_v, given_v, given_t, inverse_v, run, top, *rest
 ):
     nx, ny, nc, cap, width, sides = sizes
     rows = nx * ny
@@ -35,8 +38,10 @@
     fine = part // 2
     gathered = [rest[PARTS * l : PARTS * (l + 1)] for l in range(3)]
     rest = rest[3 * PARTS :]
-    sums, xa, y_in, ya = [[rest[4 * j + i] for j in range(3)] for i in range(4)]
-    give, take, table_sem, load_sem, small_sem, send_sem, recv_sem = rest[12:]
+    near_out, near_in, far_out, far_in, y_out, y_in, w_out, w_in = [
+        [rest[8 * l + i] for l in range(3)] for i in range(8)
+    ]
+    give, take, table_sem, out_sem, load_sem, small_sem, send_sem, recv_sem = rest[24:]
     p = lax.axis_index("prow")
     c = lax.axis_index("pcol")
     k = lax.axis_index("zgrid")
@@ -53,7 +58,8 @@
         return {"pcol": lax.rem(c + d, nc)}
 
     core = {"zgrid": 1 - k}
-    x_order = sorted(range(1, nx), key=lambda d: -min(d, nx - d))
+    near = [d for d in range(1, nx) if min(d, nx - d) == 1]
+    far = [d for d in range(1, nx) if min(d, nx - d) > 1]
     y_order = sorted(range(1, ny), key=lambda d: -min(d, ny - d))
     z_order = sorted(range(1, nc), key=lambda d: -min(d, nc - d))
     pending = {}
@@ -84,48 +90,22 @@
         i = inverse_sub.at[n] if n < 2 else inverse_top.at[n - 2]
         smalls.append(pltpu.make_async_copy(g, given_v.at[n], small_sem.at[2 * n]))
         smalls.append(pltpu.make_async_copy(i, inverse_v.at[n], small_sem.at[2 * n + 1]))
-    for s in smalls:
+    indices = [
+        pltpu.make_async_copy(a, b, index_sem.at[n])
+        for n, (a, b) in enumerate(((sources_h, sources), (counts_h, counts), (targets_h, targets)))
+    ]
+    for s in smalls[:2] + indices + smalls[2:]:
         s.start()
     for s in loads:
         s.start()
 
     barrier = pltpu.get_barrier_semaphore()
     partners = (
-        [x_peer(d) for d in x_order] + [y_peer(d) for d in y_order]
+        [x_peer(d) for d in near + far] + [y_peer(d) for d in y_order]
         + [z_peer(d) for d in z_order] + [core]
     )
     for device in partners:
         pl.semaphore_signal(barrier, inc=1, device_id=device, device_id_type=MESH)
-
-    lanes = lax.broadcasted_iota(jnp.int32, (1, LANES), 1)
-    key_v[...] = jnp.full(key_v.shape, -1, jnp.int32)
-    for l in range(3):
-        live = lanes[:, :cap] < counts[0, l]
-        key_v[l : l + 1, :cap] = jnp.where(live, targets[l], -1)
-    key_rows = key_v[...]
-    key_columns = key_rows.T
-    line = lax.broadcasted_iota(jnp.int32, (LANES, LANES), 0)
-    lane = lax.broadcasted_iota(jnp.int32, (LANES, LANES), 1)
-
-    def latest(wanted, l, strict):
-        best = jnp.full((1, LANES), -1, jnp.int32)
-        for m in range(l + 1):
-            hit = (key_columns[:, m : m + 1] == wanted) & (wanted >= 0)
-            if m == l and strict:
-                hit = hit & (line < lane)
-            best = jnp.maximum(best, jnp.max(jnp.where(hit, line + m * cap, -1), axis=0, keepdims=True))
-        return jnp.where(best < 0, slots, best)
-
-    for l in range(3):
-        table_v[l : l + 1] = latest(key_rows[l : l + 1], l, True)
-        table_v[3 + l : 4 + l] = latest(lanes + l * rows, l, False)
-    to_scalars = pltpu.make_async_copy(table_v, table, table_sem)
-    to_scalars.start()
-    run[slots] = jnp.zeros((sides, width), jnp.float32)
-    for s in smalls:
-        s.wait()
-    for n in range(4):
-        given_t[n] = given_v[n].astype(jnp.float32).T
 
     def natural(j, h):
         return pl.ds(h * part + j * fine, fine)
@@ -179,38 +159,64 @@
 
         lax.fori_loop(0, cap // group, step, 0)
 
-    def x_stage(l, j, value):
-        kept = sums[l].at[j]
-        for d in x_order:
+    def first_stage(l, j, value):
+        n = l + 1
+        for f, d in enumerate(far):
             to = lax.rem(x + d, nx)
 
-            def place(m, carry):
-                kept[d - 1, m] = value(to, m).astype(jnp.bfloat16)
+            def place_far(m, carry):
+                far_out[l][j, f, m] = value(to, m).astype(jnp.bfloat16)
                 return carry
 
-            lax.fori_loop(0, ny, place, 0)
-            send(kept.at[d - 1], xa[l].at[j, d - 1], f"x{l + 1}", j, x_peer(d), xa[l].at[j])
-
-    def y_stage(l, j, value):
-        arrive(f"x{l + 1}", j)
+            lax.fori_loop(0, ny, place_far, 0)
+            for e in y_order:
+                send(
+                    far_out[l].at[j, f, lax.rem(y + e, ny)], far_in[l].at[j, f, e - 1],
+                    f"v{n}", j, y_peer(e), far_in[l].at[j],
+                )
+        for f, d in enumerate(near):
+            to = lax.rem(x + d, nx)
+
+            def place_near(m, carry):
+                near_out[l][j, f, m] = value(to, m).astype(jnp.bfloat16)
+                return carry
+
+            lax.fori_loop(0, ny, place_near, 0)
+            send(near_out[l].at[j, f], near_in[l].at[j, f], f"x{n}", j, x_peer(d), near_in[l].at[j])
+
+    def second_stage(l, j, value):
+        n = l + 1
+        arrive(f"x{n}", j)
 
         def add(m, carry):
             total = value(x, m)
-            for d in range(nx - 1):
-                total = total + xa[l][j, d, m].astype(jnp.float32)
-            y_in[l][j, m] = total.astype(jnp.bfloat16)
+            for f in range(len(near)):
+                total = total + near_in[l][j, f, m].astype(jnp.float32)
+            y_out[l][j, m] = total.astype(jnp.bfloat16)
             return carry
 
         lax.fori_loop(0, ny, add, 0)
-        for d in y_order:
-            to = lax.rem(y + d, ny)
-            send(y_in[l].at[j, to], ya[l].at[j, d - 1], f"y{l + 1}", j, y_peer(d), ya[l].at[j])
+        for e in y_order:
+            send(y_out[l].at[j, lax.rem(y + e, ny)], y_in[l].at[j, e - 1], f"y{n}", j, y_peer(e), y_in[l].at[j])
+        if far:
+            arrive(f"v{n}", j)
+        for f, d in enumerate(far):
+            total = value(lax.rem(x + d, nx), y)
+            for e in range(ny - 1):
+                total = total + far_in[l][j, f, e].astype(jnp.float32)
+            w_out[l][j, f] = total.astype(jnp.bfloat16)
+            send(w_out[l].at[j, f], w_in[l].at[j, f], f"w{n}", j, x_peer(d), w_in[l].at[j])
 
     def incoming(l, j):
-        arrive(f"y{l + 1}", j)
-        total = y_in[l][j, y].astype(jnp.float32)
-        for d in range(ny - 1):
-            total = total + ya[l][j, d].astype(jnp.float32)
+        n = l + 1
+        arrive(f"y{n}", j)
+        total = y_out[l][j, y].astype(jnp.float32)
+        for e in range(ny - 1):
+            total = total + y_in[l][j, e].astype(jnp.float32)
+        if far:
+            arrive(f"w{n}", j)
+        for f in range(len(far)):
+            total = total + w_in[l][j, f].astype(jnp.float32)
         return total
 
     def own_value(l, lines):
@@ -244,26 +250,68 @@
         lines = pl.ds(pl.multiple_of(k * part + j * fine, fine), fine)
         return solve(l + 1, given_t[l + 1, lines] - incoming(l, j))
 
-    def emit(out, n, pieces):
+    def prepare():
+        for s in indices:
+            s.wait()
+        lanes = lax.broadcasted_iota(jnp.int32, (1, LANES), 1)
+        key_v[...] = jnp.full(key_v.shape, -1, jnp.int32)
+        for l in range(3):
+            live = lanes[:, :cap] < counts[0, l]
+            key_v[l : l + 1, :cap] = jnp.where(live, targets[l], -1)
+        key_rows = key_v[...]
+        key_columns = key_rows.T
+        line = lax.broadcasted_iota(jnp.int32, (LANES, LANES), 0)
+        lane = lax.broadcasted_iota(jnp.int32, (LANES, LANES), 1)
+
+        def latest(wanted, l, strict):
+            best = jnp.full((1, LANES), -1, jnp.int32)
+            for m in range(l + 1):
+                hit = (key_columns[:, m : m + 1] == wanted) & (wanted >= 0)
+                if m == l and strict:
+                    hit = hit & (line < lane)
+                best = jnp.maximum(best, jnp.max(jnp.where(hit, line + m * cap, -1), axis=0, keepdims=True))
+            return jnp.where(best < 0, slots, best)
+
+        for l in range(3):
+            table_v[l : l + 1] = latest(key_rows[l : l + 1], l, True)
+            table_v[3 + l : 4 + l] = latest(lanes + l * rows, l, False)
+        to_scalars = pltpu.make_async_copy(table_v, table, table_sem)
+        to_scalars.start()
+        run[slots] = jnp.zeros((sides, width), jnp.float32)
+        for l in range(1, 4):
+            smalls[2 * l].wait()
+            smalls[2 * l + 1].wait()
+            given_t[l] = given_v[l].astype(jnp.float32).T
+        turn(0)
+        to_scalars.wait()
+
+    writes = []
+
+    def emit(n, pieces):
         whole = jnp.concatenate(
             [pieces(j, h) for h in range(2) for j in range(PARTS)], axis=0
         )
-        out[n] = whole.astype(jnp.float32).T.astype(jnp.bfloat16)
-
-    to_scalars.wait()
-    turn(0)
+        result[n] = whole.astype(jnp.float32).T.astype(jnp.bfloat16)
+        out = out_sub.at[n] if n < 2 else out_top.at[n - 2]
+        writes.append(pltpu.make_async_copy(result.at[n], out, out_sem.at[n]))
+        writes[-1].start()
+
+    smalls[0].wait()
+    smalls[1].wait()
+    given_t[0] = given_v[0].astype(jnp.float32).T
+    parts = range(PARTS)
+    firsts = [solve(0, of_part(0, j)) for j in parts]
     pl.semaphore_wait(barrier, len(partners))
-
-    parts = range(PARTS)
-    for j in parts:
-        share(0, j, solve(0, of_part(0, j)))
+    for j in parts:
+        share(0, j, firsts[j])
+    prepare()
     for j in parts:
         arrive("g0", j)
         products(0, j)
-        x_stage(0, j, own_value(0, sub_lines(j)))
+        first_stage(0, j, own_value(0, sub_lines(j)))
     turn(1)
     for j in parts:
-        y_stage(0, j, own_value(0, sub_lines(j)))
+        second_stage(0, j, own_value(0, sub_lines(j)))
     for j in parts:
         share(1, j, solve(1, of_part(1, j) - incoming(0, j)))
     for j in parts:
@@ -272,10 +320,10 @@
         core_stage(1, j)
     for j in parts:
         arrive("c2", j)
-        x_stage(1, j, merged(1, j))
+        first_stage(1, j, merged(1, j))
     turn(2)
     for j in parts:
-        y_stage(1, j, merged(1, j))
+        second_stage(1, j, merged(1, j))
     for j in parts:
         held = gathered[2][j]
         solved = top_solve(1, j)
@@ -287,25 +335,45 @@
         arrive("g2", j)
         send(held.at[k], held.at[k], "f2", j, core, held.at[0])
     for n in range(2):
-        emit(out_sub, n, lambda j, h, n=n: gathered[n][j][c, pl.ds(h * fine, fine)])
+        emit(n, lambda j, h, n=n: gathered[n][j][c, pl.ds(h * fine, fine)])
     for j in parts:
         arrive("f2", j)
         products(2, j)
         core_stage(2, j)
     for j in parts:
         arrive("c3", j)
-        x_stage(2, j, merged(2, j))
-    for j in parts:
-        y_stage(2, j, merged(2, j))
-    emit(out_top, 0, lambda j, h: gathered[2][j][h, c])
+        first_stage(2, j, merged(2, j))
+    for j in parts:
+        second_stage(2, j, merged(2, j))
+    emit(2, lambda j, h: gathered[2][j][h, c])
     for j in parts:
         solved = top_solve(2, j)
         top[j, k] = solved
         send(top.at[j, k], top.at[j, k], "f3", j, core, top.at[j, 0])
     for j in parts:
         arrive("f3", j)
-    emit(out_top, 1, lambda j, h: top[j, h])
+    emit(3, lambda j, h: top[j, h])
+    for w in writes:
+        w.wait()
     finish()
+
+
+def copy_kernel(sub, top, out_sub, out_top, sub_v, top_v, sems):
+    reads = (
+        pltpu.make_async_copy(sub, sub_v, sems.at[0]),
+        pltpu.make_async_copy(top, top_v, sems.at[1]),
+    )
+    writes = (
+        pltpu.make_async_copy(sub_v, out_sub, sems.at[2]),
+        pltpu.make_async_copy(top_v, out_top, sems.at[3]),
+    )
+    for r in reads:
+        r.start()
+    for r, w in zip(reads, writes):
+        r.wait()
+        w.start()
+    for w in writes:
+        w.wait()
 
 
 def local(nx, axis_sizes, blocks, sources, targets, counts, given_sub, given_top, inverse_sub, inverse_top):
@@ -318,17 +386,23 @@
     sizes = (nx, ny, nc, cap, width, sides)
     bf16 = jnp.bfloat16
 
+    near = min(2, nx - 1)
+    far = nx - 1 - near
+
     def exchange(height):
+        block = (height, width)
         return [
-            pltpu.VMEM((PARTS, nx - 1, ny, height, width), bf16),
-            pltpu.VMEM((PARTS, nx - 1, ny, height, width), bf16),
-            pltpu.VMEM((PARTS, ny, height, width), bf16),
-            pltpu.VMEM((PARTS, ny - 1, height, width), bf16),
+            pltpu.VMEM((PARTS, near, ny) + block, bf16),
+            pltpu.VMEM((PARTS, near, ny) + block, bf16),
+            pltpu.VMEM((PARTS, max(far, 1), ny) + block, bf16),
+            pltpu.VMEM((PARTS, max(far, 1), ny - 1) + block, bf16),
+            pltpu.VMEM((PARTS, ny) + block, bf16),
+            pltpu.VMEM((PARTS, ny - 1) + block, bf16),
+            pltpu.VMEM((PARTS, max(far, 1)) + block, bf16),
+            pltpu.VMEM((PARTS, max(far, 1)) + block, bf16),
         ]
 
-    smem = pl.BlockSpec(memory_space=pltpu.SMEM)
     anywhere = pl.BlockSpec(memory_space=pltpu.HBM)
-    vmem = pl.BlockSpec(memory_space=pltpu.VMEM)
     semaphores = len(STEPS) * PARTS
     solved_sub, solved_top = pl.pallas_call(
         functools.partial(kernel, sizes),
@@ -336,9 +410,14 @@
             jax.ShapeDtypeStruct((2, width, sides), bf16),
             jax.ShapeDtypeStruct((2, width, sides), bf16),
         ),
-        in_specs=[smem, smem, vmem] + [anywhere] * 5,
-        out_specs=(vmem, vmem),
+        in_specs=[anywhere] * 8,
+        out_specs=(anywhere, anywhere),
         scratch_shapes=[
+            pltpu.SMEM((levels, 1, cap), jnp.int32),
+            pltpu.SMEM((1, levels), jnp.int32),
+            pltpu.VMEM((levels, 1, cap), jnp.int32),
+            pltpu.SemaphoreType.DMA((3,)),
+            pltpu.VMEM((4, width, sides), bf16),
             pltpu.VMEM((8, LANES), jnp.int32),
             pltpu.VMEM((8, LANES), jnp.int32),
             pltpu.SMEM((8, LANES), jnp.int32),
@@ -356,6 +435,7 @@
             pltpu.VMEM((2, PARTS, ny, nx, fine, width), bf16),
             pltpu.VMEM((2, PARTS, ny, nx, fine, width), bf16),
             pltpu.SemaphoreType.DMA,
+            pltpu.SemaphoreType.DMA((4,)),
             pltpu.SemaphoreType.DMA((3,)),
             pltpu.SemaphoreType.DMA((8,)),
             pltpu.SemaphoreType.DMA((semaphores,)),
@@ -369,6 +449,22 @@
         sources.reshape(levels, 1, cap), counts.reshape(1, levels), targets.reshape(levels, 1, cap), blocks[0, 0, 0], given_sub[0, 0, 0], given_top[0, 0],
         inverse_sub[0, 0, 0], inverse_top[0, 0],
     )
+    solved_sub, solved_top = pl.pallas_call(
+        copy_kernel,
+        out_shape=(
+            jax.ShapeDtypeStruct((2, width, sides), bf16),
+            jax.ShapeDtypeStruct((2, width, sides), bf16),
+        ),
+        in_specs=[anywhere] * 2,
+        out_specs=(anywhere, anywhere),
+        scratch_shapes=[
+            pltpu.VMEM((2, width, sides), bf16),
+            pltpu.VMEM((2, width, sides), bf16),
+            pltpu.SemaphoreType.DMA((4,)),
+        ],
+        compiler_params=pltpu.CompilerParams(vmem_limit_bytes=60 * 1024 * 1024),
+        name="hand_over",
+    )(solved_sub, solved_top)
     return solved_sub[None, None, None], solved_top[None, None]
 
 

time: 86 us -> 75.2 us (0.87)
  Pallas kernels: 82.2 us -> 74.4 us
  local copies, waits for them, and re-layouts: 2.95 us -> 0 us
    pallas_call x1, Pallas kernels: 82.2 us -> 72.9 us  [local(): pl.pallas_call(functools.partial(kernel, sizes), out_shape=(jax.ShapeDtyp...]
    unnamed x2 -> x0, local copies, waits for them, and re-layouts: 2.95 us -> none
    pallas_call x0 -> x1, Pallas kernels: none -> 1.53 us  [local(): pl.pallas_call(copy_kernel, out_shape=(jax.ShapeDtypeStruct((2, width, si...]
where the time goes in v3:
time: 75.2 us; the launch traced here: 75 us
  Pallas kernels  74.4 us (99%)
    pallas_call x1, Pallas kernels, local(): pl.pallas_call(functools.partial(kernel, sizes), out_shape=(jax.ShapeDtyp...  72.9 us
    pallas_call x1, Pallas kernels, local(): pl.pallas_call(copy_kernel, out_shape=(jax.ShapeDtypeStruct((2, width, si...  1.53 us

profile of v3, /device:TPU:1, one launch (start us, length us, event | category | flops | bytes accessed | tf_op | source)
XLA Modules:
  0.0 75.0 jit_solution(1952473141928208133)
XLA Ops:
  0.6 72.9 %substitution.1 = (bf16[2,128,128]{2,1,0:T(8,128)(2,1)}, bf16[2,128,128]{2,1,0:T(8,128)(2,1)}) custom-call(s32[3,1,40]{2,1,0:T(1,128)} %bitcast.15, s32[1,3]{1,0:T(1,128)} %bitcast.17, s32[3,1,40]{2,1,0:T(1,128)} %bitcast.16, bf16[3,40,128,128]{3,2,1,0:T(8,128)(2,1)} %bitcast.10, bf16[2,128,128]{2,1,0:T(8,128)(2,1)} %bitcast.11, ...), custom_call_target="tpu_custom_call" | custom-call | tf_op jit(solution)/shard_map/substitution/pallas_call | solution.py:407
  73.5 1.5 %hand_over.1 = (bf16[2,128,128]{2,1,0:T(8,128)(2,1)}, bf16[2,128,128]{2,1,0:T(8,128)(2,1)}) custom-call(bf16[2,128,128]{2,1,0:T(8,128)(2,1)} %get-tuple-element.6.sub, bf16[2,128,128]{2,1,0:T(8,128)(2,1)} %get-tuple-element.7.top), custom_call_target="tpu_custom_call" | custom-call | tf_op jit(solution)/shard_map/hand_over/pallas_call | solution.py:452

commit v4 on v3

--- a/solution.py
+++ b/solution.py
@@ -9,11 +9,11 @@
 
 MESH = pl.DeviceIdType.MESH
 X_CHIPS = 4
-PARTS = 2
+PARTS = 4
 LANES = 128
 STEPS = (
-    "g0", "x1", "v1", "y1", "w1", "g1", "c2", "x2", "v2", "y2", "w2", "g2", "f2",
-    "c3", "x3", "v3", "y3", "w3", "f3",
+    "g0", "x1", "v1", "y1", "w1", "g1", "x2", "v2", "y2", "w2", "g2", "f2",
+    "x3", "v3", "y3", "w3", "f3",
 )
 
 
@@ -41,7 +41,7 @@
     near_out, near_in, far_out, far_in, y_out, y_in, w_out, w_in = [
         [rest[8 * l + i] for l in range(3)] for i in range(8)
     ]
-    give, take, table_sem, out_sem, load_sem, small_sem, send_sem, recv_sem = rest[24:]
+    own_out, table_sem, out_sem, load_sem, small_sem, send_sem, recv_sem = rest[24:]
     p = lax.axis_index("prow")
     c = lax.axis_index("pcol")
     k = lax.axis_index("zgrid")
@@ -58,6 +58,13 @@
         return {"pcol": lax.rem(c + d, nc)}
 
     core = {"zgrid": 1 - k}
+
+    def across(device):
+        return dict(device, zgrid=1 - k)
+
+    def on_core(device, h):
+        return dict(device, zgrid=h)
+
     near = [d for d in range(1, nx) if min(d, nx - d) == 1]
     far = [d for d in range(1, nx) if min(d, nx - d) > 1]
     y_order = sorted(range(1, ny), key=lambda d: -min(d, ny - d))
@@ -101,14 +108,15 @@
 
     barrier = pltpu.get_barrier_semaphore()
     partners = (
-        [x_peer(d) for d in near + far] + [y_peer(d) for d in y_order]
+        [x_peer(d) for d in near + far] + [across(x_peer(d)) for d in near]
+        + [y_peer(d) for d in y_order] + [across(y_peer(d)) for d in (y_order if far else [])]
         + [z_peer(d) for d in z_order] + [core]
     )
     for device in partners:
         pl.semaphore_signal(barrier, inc=1, device_id=device, device_id_type=MESH)
 
     def natural(j, h):
-        return pl.ds(h * part + j * fine, fine)
+        return pl.ds(h * (sides // 2) + j * fine, fine)
 
     def of_part(l, j):
         return jnp.concatenate([given_t[l, natural(j, h)] for h in range(2)], axis=0)
@@ -184,13 +192,54 @@
             lax.fori_loop(0, ny, place_near, 0)
             send(near_out[l].at[j, f], near_in[l].at[j, f], f"x{n}", j, x_peer(d), near_in[l].at[j])
 
+    def first_stage_top(l, j):
+        n = l + 1
+        lines = sub_lines(j)
+
+        def split(kept, to):
+            def place(m, carry):
+                block = run[table[3 + l, m * nx + to], lines].astype(jnp.bfloat16)
+                kept[0, m] = block[:fine]
+                kept[1, m] = block[fine:]
+                return carry
+
+            lax.fori_loop(0, ny, place, 0)
+
+        for f, d in enumerate(far):
+            kept = far_out[l].at[j, f]
+            split(kept, lax.rem(x + d, nx))
+            for e in y_order:
+                for h in range(2):
+                    send(
+                        kept.at[h, lax.rem(y + e, ny)], far_in[l].at[j, f, k * (ny - 1) + e - 1],
+                        f"v{n}", j, on_core(y_peer(e), h), far_in[l].at[j],
+                    )
+            send(kept.at[1 - k, y], far_in[l].at[j, f, 2 * (ny - 1)], f"v{n}", j, core, far_in[l].at[j])
+        for f, d in enumerate(near):
+            kept = near_out[l].at[j, f]
+            split(kept, lax.rem(x + d, nx))
+            for h in range(2):
+                send(
+                    kept.at[h], near_in[l].at[j, 2 * f + k], f"x{n}", j,
+                    on_core(x_peer(d), h), near_in[l].at[j],
+                )
+
+        def place_own(m, carry):
+            own_out[l - 1, j, m] = run[table[3 + l, m * nx + x], top_lines(j, 1 - k)].astype(jnp.bfloat16)
+            return carry
+
+        lax.fori_loop(0, ny, place_own, 0)
+        send(own_out.at[l - 1, j], near_in[l].at[j, 2 * len(near)], f"x{n}", j, core, near_in[l].at[j])
+
     def second_stage(l, j, value):
         n = l + 1
         arrive(f"x{n}", j)
+        near_count = len(near) if l == 0 else 2 * len(near) + 1
+        far_count = ny - 1 if l == 0 else 2 * (ny - 1) + 1
 
         def add(m, carry):
             total = value(x, m)
-            for f in range(len(near)):
+            for f in range(near_count):
                 total = total + near_in[l][j, f, m].astype(jnp.float32)
             y_out[l][j, m] = total.astype(jnp.bfloat16)
             return carry
@@ -202,7 +251,7 @@
             arrive(f"v{n}", j)
         for f, d in enumerate(far):
             total = value(lax.rem(x + d, nx), y)
-            for e in range(ny - 1):
+            for e in range(far_count):
                 total = total + far_in[l][j, f, e].astype(jnp.float32)
             w_out[l][j, f] = total.astype(jnp.bfloat16)
             send(w_out[l].at[j, f], w_in[l].at[j, f], f"w{n}", j, x_peer(d), w_in[l].at[j])
@@ -228,26 +277,8 @@
     def top_lines(j, h):
         return pl.ds(pl.multiple_of(j * part + h * fine, fine), fine)
 
-    def merged(l, j):
-        def value(to, m):
-            own = run[table[3 + l, m * nx + to], top_lines(j, k)]
-            return own + take[l - 1, j, m, to].astype(jnp.float32)
-
-        return value
-
-    def core_stage(l, j):
-        kept = give.at[l - 1, j]
-
-        def place(m, carry):
-            for to in range(nx):
-                kept[m, to] = run[table[3 + l, m * nx + to], top_lines(j, 1 - k)].astype(jnp.bfloat16)
-            return carry
-
-        lax.fori_loop(0, ny, place, 0)
-        send(kept, take.at[l - 1, j], f"c{l + 1}", j, core, take.at[l - 1, j])
-
     def top_solve(l, j):
-        lines = pl.ds(pl.multiple_of(k * part + j * fine, fine), fine)
+        lines = pl.ds(pl.multiple_of(k * (sides // 2) + j * fine, fine), fine)
         return solve(l + 1, given_t[l + 1, lines] - incoming(l, j))
 
     def prepare():
@@ -317,13 +348,10 @@
     for j in parts:
         arrive("g1", j)
         products(1, j)
-        core_stage(1, j)
-    for j in parts:
-        arrive("c2", j)
-        first_stage(1, j, merged(1, j))
+        first_stage_top(1, j)
     turn(2)
     for j in parts:
-        second_stage(1, j, merged(1, j))
+        second_stage(1, j, own_value(1, top_lines(j, k)))
     for j in parts:
         held = gathered[2][j]
         solved = top_solve(1, j)
@@ -339,12 +367,9 @@
     for j in parts:
         arrive("f2", j)
         products(2, j)
-        core_stage(2, j)
-    for j in parts:
-        arrive("c3", j)
-        first_stage(2, j, merged(2, j))
-    for j in parts:
-        second_stage(2, j, merged(2, j))
+        first_stage_top(2, j)
+    for j in parts:
+        second_stage(2, j, own_value(2, top_lines(j, k)))
     emit(2, lambda j, h: gathered[2][j][h, c])
     for j in parts:
         solved = top_solve(2, j)
@@ -389,13 +414,14 @@
     near = min(2, nx - 1)
     far = nx - 1 - near
 
-    def exchange(height):
+    def exchange(height, split):
         block = (height, width)
+        halves = (2,) if split else ()
         return [
-            pltpu.VMEM((PARTS, near, ny) + block, bf16),
-            pltpu.VMEM((PARTS, near, ny) + block, bf16),
-            pltpu.VMEM((PARTS, max(far, 1), ny) + block, bf16),
-            pltpu.VMEM((PARTS, max(far, 1), ny - 1) + block, bf16),
+            pltpu.VMEM((PARTS, near) + halves + (ny,) + block, bf16),
+            pltpu.VMEM((PARTS, 2 * near + 1 if split else near, ny) + block, bf16),
+            pltpu.VMEM((PARTS, max(far, 1)) + halves + (ny,) + block, bf16),
+            pltpu.VMEM((PARTS, max(far, 1), 2 * ny - 1 if split else ny - 1) + block, bf16),
             pltpu.VMEM((PARTS, ny) + block, bf16),
             pltpu.VMEM((PARTS, ny - 1) + block, bf16),
             pltpu.VMEM((PARTS, max(far, 1)) + block, bf16),
@@ -429,11 +455,10 @@
             pltpu.VMEM((PARTS, 2, fine, width), bf16),
             *[pltpu.VMEM((nc, part, width), bf16)] * (2 * PARTS),
             *[pltpu.VMEM((2, nc, fine, width), bf16)] * PARTS,
-            *exchange(part),
-            *exchange(fine),
-            *exchange(fine),
-            pltpu.VMEM((2, PARTS, ny, nx, fine, width), bf16),
-            pltpu.VMEM((2, PARTS, ny, nx, fine, width), bf16),
+            *exchange(part, False),
+            *exchange(fine, True),
+            *exchange(fine, True),
+            pltpu.VMEM((2, PARTS, ny, fine, width), bf16),
             pltpu.SemaphoreType.DMA,
             pltpu.SemaphoreType.DMA((4,)),
             pltpu.SemaphoreType.DMA((3,)),

time: 75.2 us -> 73.4 us (0.976)
  Pallas kernels: 74.4 us -> 72.6 us
    pallas_call x1, Pallas kernels: 72.9 us -> 71 us  [local(): pl.pallas_call(functools.partial(kernel, sizes), out_shape=(jax.ShapeDtyp...]
where the time goes in v4:
time: 73.4 us; the launch traced here: 73.2 us
  Pallas kernels  72.6 us (99%)
    pallas_call x1, Pallas kernels, local(): pl.pallas_call(functools.partial(kernel, sizes), out_shape=(jax.ShapeDtyp...  71 us
    pallas_call x1, Pallas kernels, local(): pl.pallas_call(copy_kernel, out_shape=(jax.ShapeDtypeStruct((2, width, si...  1.53 us

profile of v4, /device:TPU:1, one launch (start us, length us, event | category | flops | bytes accessed | tf_op | source)
XLA Modules:
  0.0 73.2 jit_solution(838733691567950331)
XLA Ops:
  0.6 71.0 %substitution.1 = (bf16[2,128,128]{2,1,0:T(8,128)(2,1)}, bf16[2,128,128]{2,1,0:T(8,128)(2,1)}) custom-call(s32[3,1,40]{2,1,0:T(1,128)} %bitcast.15, s32[1,3]{1,0:T(1,128)} %bitcast.17, s32[3,1,40]{2,1,0:T(1,128)} %bitcast.16, bf16[3,40,128,128]{3,2,1,0:T(8,128)(2,1)} %bitcast.10, bf16[2,128,128]{2,1,0:T(8,128)(2,1)} %bitcast.11, ...), custom_call_target="tpu_custom_call" | custom-call | tf_op jit(solution)/shard_map/substitution/pallas_call | solution.py:433
  71.7 1.5 %hand_over.1 = (bf16[2,128,128]{2,1,0:T(8,128)(2,1)}, bf16[2,128,128]{2,1,0:T(8,128)(2,1)}) custom-call(bf16[2,128,128]{2,1,0:T(8,128)(2,1)} %get-tuple-element.6.sub, bf16[2,128,128]{2,1,0:T(8,128)(2,1)} %get-tuple-element.7.top), custom_call_target="tpu_custom_call" | custom-call | tf_op jit(solution)/shard_map/hand_over/pallas_call | solution.py:477
